TPU v7x, 32 devices: a whole 2x2x4 slice. The times are simulated.
32 devices in a mesh: row: 4 (over y, core), col: 8 (over z, x).
Axes of the slice: x: 2, y: 2, z: 4, core: 2. Of those that a mesh axis runs over, the one named last changes fastest.
Arguments:
- fock: float32 [2, 8192, 8192], P(None, 'row', 'col'), may hold values from -1.1875 to 1.1875, as said below
- density: float32 [2, 8192, 8192], P(None, 'row', 'col'), may hold values from -1.09375 to 1.09375, as said below
- probe: float32 [2, 8192, 128], P(None, 'col'), may hold values from -6 to 6
Outputs:
- propagated: float32 [2, 8192, 128], P(None, 'col')
Inputs may be any that keep to these rules, and one draw needn't show every extreme that they name: Hermitian: fock[0] is symmetric and fock[1] antisymmetric, exactly. Hermitian: density[0] is symmetric and density[1] antisymmetric, exactly.
All inputs are finite; a program needn't handle non-finite values.
Results may differ from a plain program's by a relative error of at most 0.00011.
Values sent between devices are 32-bit elements; how exact they have to be, the bound alone decides.
A program may use at most 128 MiB of HBM per device.

v0:
```python
import jax
import jax.numpy as jnp
from jax import lax
from jax.sharding import PartitionSpec as P

time_step = 0.5


def broadcast(block, axis, owner):
    block = jnp.where(lax.axis_index(axis) == owner, block, jnp.zeros_like(block))
    return lax.psum(block, axis)


def plain_dot(left, right):
    return jnp.dot(left, right, precision=lax.Precision.HIGHEST, preferred_element_type=jnp.float32)


def adjoint_dot(left, right):
    return lax.dot_general(
        left,
        right,
        (((0,), (0,)), ((), ())),
        precision=lax.Precision.HIGHEST,
        preferred_element_type=jnp.float32,
    )


def prepare(matrix, adjoint):
    real_m = matrix[0]
    imag_m = -matrix[1] if adjoint else matrix[1]
    return (real_m, imag_m, real_m + imag_m, imag_m - real_m)


def complex_product(pieces, vector, adjoint):
    multiply = adjoint_dot if adjoint else plain_dot
    real_m, imag_m, sum_m, diff_m = pieces
    real_v = vector[0]
    imag_v = vector[1]
    real_part = multiply(real_m, real_v) - multiply(imag_m, imag_v)
    imag_part = multiply(real_m, imag_v) + multiply(imag_m, real_v)
    return jnp.stack([real_part, imag_part])


def times_imag(vector, factor):
    return jnp.stack([-factor * vector[1], factor * vector[0]])


def shards(fock, density, probe):
    rows_block = fock.shape[1]
    cols_block = fock.shape[2]
    fock_plain = prepare(fock, False)
    fock_adjoint = prepare(fock, True)
    density_plain = prepare(density, False)

    def reduce_cols(partial_value):
        share = lax.psum_scatter(partial_value, "col", scatter_dimension=1, tiled=True)
        return lax.all_gather(share, "col", axis=1, tiled=True)

    def to_columns(vector):
        column = lax.axis_index("col")
        source = column * cols_block // rows_block
        offset = column * cols_block - source * rows_block
        piece = lax.dynamic_slice_in_dim(vector, offset, cols_block, 1)
        return broadcast(piece, "row", source)

    def forward(pieces, vector):
        return reduce_cols(complex_product(pieces, vector, False))

    def backward(pieces, vector):
        return lax.psum(complex_product(pieces, vector, True), "row")

    def alternate(vector, in_columns, sign):
        current = vector
        column_sum = vector if in_columns else None
        row_sum = None if in_columns else vector
        if in_columns:
            current = forward(fock_plain, current)
        else:
            current = backward(fock_adjoint, current)
        in_columns = not in_columns
        current = times_imag(current, sign * time_step / 1)
        if in_columns:
            column_sum = current
        else:
            row_sum = current
        return (column_sum, row_sum)

    column_sum, row_sum = alternate(probe, True, 1.0)
    first = column_sum + to_columns(row_sum)
    second = forward(density_plain, first)
    column_sum, row_sum = alternate(second, False, -1.0)
    result = column_sum + to_columns(row_sum)
    return result


def solution(mesh):
    return jax.shard_map(
        shards,
        mesh=mesh,
        in_specs=(P(None, "row", "col"), P(None, "row", "col"), P(None, "col", None)),
        out_specs=P(None, "col", None),
        check_vma=False,
    )
```

profile of v0, /device:TPU:0, one launch (start us, length us, event | category | flops | bytes accessed | tf_op | source)
XLA Modules:
  0.0 483.9 jit_solution(5224947570114361618)
XLA Ops:
  6.5 0.0 reduce-scatter.3.cloned.1.call-start
  6.5 9.3 %fusion.12 = f32[2048,128]{1,0:T(8,128)S(1)} fusion(f32[2,2048,1024]{2,1,0:T(8,128)} %param.3, f32[2,1024,128]{2,1,0:T(8,128)} %param.5), kind=kOutput, calls=%fused_computation.12 | convolution fusion | flops 3221225472 | bytes 9961472 | tf_op jit(solution)/shard_map/dot_general | solution.py:15
  15.9 0.0 copy-done.2
  15.9 9.5 %fusion.14 = f32[2048,128]{1,0:T(8,128)S(1)} fusion(f32[2,2048,1024]{2,1,0:T(8,128)} %param.3, f32[2,1024,128]{2,1,0:T(8,128)S(1)} %copy-done.2), kind=kOutput, calls=%fused_computation.14 | convolution fusion | flops 3221225472 | bytes 9961472 | tf_op jit(solution)/shard_map/dot_general | solution.py:15
  25.4 0.0 copy-done
  25.4 7.0 %fusion.47 = f32[1,2048,128]{2,1,0:T(8,128)S(1)} fusion(f32[2048,128]{1,0:T(8,128)S(1)} %fusion.12, f32[2,2048,1024]{2,1,0:T(8,128)S(1)} %copy-done, f32[2,1024,128]{2,1,0:T(8,128)S(1)} %copy-done.2), kind=kOutput, calls=%fused_computation.41 | convolution fusion | flops 3221487616 | bytes 11010048 | tf_op jit(solution)/shard_map/dot_general | solution.py:15
  32.4 7.2 %fusion.41 = f32[1,2048,128]{2,1,0:T(8,128)S(1)} fusion(f32[2048,128]{1,0:T(8,128)S(1)} %fusion.14, f32[2,2048,1024]{2,1,0:T(8,128)S(1)} %copy-done, f32[2,1024,128]{2,1,0:T(8,128)S(1)} %copy-done.2), kind=kOutput, calls=%fused_computation.39 | convolution fusion | flops 3221487616 | bytes 11010048 | tf_op jit(solution)/shard_map/dot_general | solution.py:15
  39.7 1.5 pad_maximum_fusion
  41.2 0.0 reduce-scatter.3.cloned.1.call-update
  41.2 0.0 all-gather.3.cloned.1.call-start
  41.2 71.1 %reduce-scatter.3.cloned.1.call-done = f32[2,256,128]{2,1,0:T(8,128)} async-done(((f32[2,2048,128]{2,1,0:T(8,128)}), f32[2,256,128]{2,1,0:T(8,128)}) %reduce-scatter.3.cloned.1.call-update) | async-done | bytes 262160 | tf_op jit(solution)/shard_map/reduce_scatter | solution.py:56
  112.4 0.0 all-gather.3.cloned.1.call-update
  112.4 0.0 all-reduce.4.cloned.1.call-start
  112.5 50.3 %all-gather.3.cloned.1.call-done = f32[2,2048,128]{2,1,0:T(8,128)} async-done(((f32[2,256,128]{2,1,0:T(8,128)}), f32[2,2048,128]{2,1,0:T(8,128)}) %all-gather.3.cloned.1.call-update) | async-done | bytes 2097168 | tf_op jit(solution)/shard_map/all_gather | solution.py:57
  162.7 1.7 slice_multiply_fusion
  164.4 1.0 fusion.75
  165.4 0.0 all-reduce.4.cloned.1.call-update
  165.5 0.0 reduce-scatter.5.cloned.1.call-start
  165.5 35.0 %all-reduce.4.cloned.1.call-done = f32[2,1024,128]{2,1,0:T(8,128)} async-done(((f32[2,1024,128]{2,1,0:T(8,128)}), f32[2,1024,128]{2,1,0:T(8,128)}) %all-reduce.4.cloned.1.call-update) | async-done | bytes 1048592 | tf_op jit(solution)/shard_map/psum | solution.py:11
  200.5 1.3 add.38
  201.8 0.0 slice-start.4
  201.8 0.0 slice-start.5
  201.8 9.2 %fusion.4 = f32[128,2048]{0,1:T(8,128)S(1)} fusion(f32[2,2048,1024]{2,1,0:T(8,128)} %param.4, f32[2,1024,128]{2,1,0:T(8,128)S(1)} %add.38), kind=kOutput, calls=%fused_computation.4 | convolution fusion | flops 3221225472 | bytes 9961472 | tf_op jit(solution)/shard_map/dot_general | solution.py:15
  211.1 0.0 slice-start.6
  211.1 10.0 %fusion.6 = f32[128,2048]{0,1:T(8,128)S(1)} fusion(f32[2,2048,1024]{2,1,0:T(8,128)} %param.4, f32[2,1024,128]{2,1,0:T(8,128)S(1)} %add.38), kind=kOutput, calls=%fused_computation.6 | convolution fusion | flops 3221225472 | bytes 9961472 | tf_op jit(solution)/shard_map/dot_general | solution.py:15
  221.1 0.0 slice-start.7
  221.1 9.5 %fusion.59 = f32[1,2048,128]{2,1,0:T(8,128)S(1)} fusion(f32[128,2048]{0,1:T(8,128)S(1)} %fusion.4, f32[2,2048,1024]{2,1,0:T(8,128)} %param.4, f32[2,1024,128]{2,1,0:T(8,128)S(1)} %add.38), kind=kOutput, calls=%fused_computation.45 | convolution fusion | flops 3221487616 | bytes 11010048 | tf_op jit(solution)/shard_map/dot_general | solution.py:15
  230.6 0.0 slice-done.4
  230.6 0.0 slice-done.5
  230.7 7.1 %fusion.53 = f32[1,2048,128]{2,1,0:T(8,128)S(1)} fusion(f32[128,2048]{0,1:T(8,128)S(1)} %fusion.6, f32[2,2048,1024]{2,1,0:T(8,128)S(1)} %bitcast.102, f32[2,1024,128]{2,1,0:T(8,128)S(1)} %add.38), kind=kOutput, calls=%fused_computation.43 | convolution fusion | flops 3221487616 | bytes 11010048 | tf_op jit(solution)/shard_map/dot_general | solution.py:15
  237.8 1.5 pad_maximum_fusion.1
  239.3 0.0 reduce-scatter.5.cloned.1.call-update
  239.3 0.0 all-gather.5.cloned.1.call-start
  239.4 68.8 %reduce-scatter.5.cloned.1.call-done = f32[2,256,128]{2,1,0:T(8,128)} async-done(((f32[2,2048,128]{2,1,0:T(8,128)}), f32[2,256,128]{2,1,0:T(8,128)}) %reduce-scatter.5.cloned.1.call-update) | async-done | bytes 262160 | tf_op jit(solution)/shard_map/reduce_scatter | solution.py:56
  308.2 0.0 all-gather.5.cloned.1.call-update
  308.3 0.0 all-reduce.6.cloned.1.call-start
  308.3 50.2 %all-gather.5.cloned.1.call-done = f32[2,2048,128]{2,1,0:T(8,128)} async-done(((f32[2,256,128]{2,1,0:T(8,128)}), f32[2,2048,128]{2,1,0:T(8,128)}) %all-gather.5.cloned.1.call-update) | async-done | bytes 2097168 | tf_op jit(solution)/shard_map/all_gather | solution.py:57
  358.5 16.1 %fusion = f32[128,1024]{0,1:T(8,128)S(1)} fusion(f32[2,2048,1024]{2,1,0:T(8,128)} %param.3, f32[2,2048,128]{2,1,0:T(8,128)} %all-gather.5.cloned.1.call-done), kind=kOutput, calls=%fused_computation | convolution fusion | flops 3223322624 | bytes 9961472 | tf_op jit(solution)/shard_map/dot_general | solution.py:19
  374.6 0.0 slice-start.2
  374.6 17.3 %fusion.2 = f32[128,1024]{0,1:T(8,128)S(1)} fusion(f32[2,2048,1024]{2,1,0:T(8,128)} %param.3, f32[2,2048,128]{2,1,0:T(8,128)} %all-gather.5.cloned.1.call-done), kind=kOutput, calls=%fused_computation.2 | convolution fusion | flops 3223322624 | bytes 9961472 | tf_op jit(solution)/shard_map/dot_general | solution.py:19
  391.9 0.0 slice-start.3
  391.9 16.2 %fusion.68 = f32[1,1024,128]{2,1,0:T(8,128)S(1)} fusion(f32[128,1024]{0,1:T(8,128)S(1)} %fusion, f32[2,2048,1024]{2,1,0:T(8,128)} %param.3, f32[2,2048,128]{2,1,0:T(8,128)S(1)} %copy-done.1), kind=kOutput, calls=%fused_computation.52 | convolution fusion | flops 3221356544 | bytes 10485760 | tf_op jit(solution)/shard_map/dot_general | solution.py:19
  408.2 13.4 %fusion.71 = f32[1,1024,128]{2,1,0:T(8,128)S(1)} fusion(f32[128,1024]{0,1:T(8,128)S(1)} %fusion.2, f32[2,2048,1024]{2,1,0:T(8,128)S(1)} %bitcast.100, f32[2,2048,128]{2,1,0:T(8,128)S(1)} %copy-done.1), kind=kOutput, calls=%fused_computation.53 | convolution fusion | flops 3221356544 | bytes 10485760 | tf_op jit(solution)/shard_map/dot_general | solution.py:19
  421.7 1.5 pad_maximum_fusion.2
  423.2 0.0 all-reduce.6.cloned.1.call-update
  423.2 50.1 %all-reduce.6.cloned.1.call-done = (f32[2,1024,128]{2,1,0:T(8,128)}, f32[2,1024,128]{2,1,0:T(8,128)}) async-done(((f32[2,1024,128]{2,1,0:T(8,128)}, f32[2,1024,128]{2,1,0:T(8,128)}), (f32[2,1024,128]{2,1,0:T(8,128)}, f32[2,1024,128]{2,1,0:T(8,128)})) %all-reduce.6.cloned.1.call-update) | async-done | bytes 2097168 | tf_op jit(solution)/shard_map/psum | solution.py:11
  473.3 1.3 slice_multiply_fusion.3
  474.6 2.3 maximum_add_fusion
  (14 shorter events, 0.0 us)
Async XLA Ops:
  6.5 9.3 %copy-start.2 = (f32[2,1024,128]{2,1,0:T(8,128)S(1)}, f32[2,1024,128]{2,1,0:T(8,128)}, u32[]{:S(2)}) copy-start(f32[2,1024,128]{2,1,0:T(8,128)} %param.5) | copy-start | bytes 3145732
  6.5 105.8 %reduce-scatter.3.cloned.1.call-start = ((), (), s32[]{:S(2)}) async-start(), calls=%async_computation.2 | async-start | bytes 2359296 | tf_op jit(solution)/shard_map/reduce_scatter | solution.py:56
  6.5 18.9 %copy-start = (f32[2,2048,1024]{2,1,0:T(8,128)S(1)}, f32[2,2048,1024]{2,1,0:T(8,128)}, u32[]{:S(2)}) copy-start(f32[2,2048,1024]{2,1,0:T(8,128)} %param.3) | copy-start | bytes 50331652
  41.2 121.5 %all-gather.3.cloned.1.call-start = ((), (), s32[]{:S(2)}) async-start(), calls=%async_computation.3 | async-start | bytes 2359296 | tf_op jit(solution)/shard_map/all_gather | solution.py:57
  112.4 88.1 %all-reduce.4.cloned.1.call-start = ((), (), s32[]{:S(2)}) async-start(), calls=%async_computation.4 | async-start | bytes 2097152 | tf_op jit(solution)/shard_map/psum | solution.py:11
  165.5 142.8 %reduce-scatter.5.cloned.1.call-start = ((), (), s32[]{:S(2)}) async-start(), calls=%async_computation.5 | async-start | bytes 2359296 | tf_op jit(solution)/shard_map/reduce_scatter | solution.py:56
  201.8 28.8 %slice-start.4 = ((s8[16777216]{0:T(1024)(128)(4,1)}), s8[4194304]{0:T(1024)(128)(4,1)S(1)}, s32[]{:S(2)}) async-start(s8[16777216]{0:T(1024)(128)(4,1)} %bitcast.101), calls=%async_computation.12 | async-start | bytes 8388608
  201.8 28.8 %slice-start.5 = ((s8[16777216]{0:T(1024)(128)(4,1)}), s8[4194304]{0:T(1024)(128)(4,1)S(1)}, s32[]{:S(2)}) async-start(s8[16777216]{0:T(1024)(128)(4,1)} %bitcast.101), calls=%async_computation.13 | async-start | bytes 8388608
  211.1 19.6 %slice-start.6 = ((s8[16777216]{0:T(1024)(128)(4,1)}), s8[4194304]{0:T(1024)(128)(4,1)S(1)}, s32[]{:S(2)}) async-start(s8[16777216]{0:T(1024)(128)(4,1)} %bitcast.101), calls=%async_computation.14 | async-start | bytes 8388608
  221.1 9.6 %slice-start.7 = ((s8[16777216]{0:T(1024)(128)(4,1)}), s8[4194304]{0:T(1024)(128)(4,1)S(1)}, s32[]{:S(2)}) async-start(s8[16777216]{0:T(1024)(128)(4,1)} %bitcast.101), calls=%async_computation.15 | async-start | bytes 8388608
  239.3 119.1 %all-gather.5.cloned.1.call-start = ((), (), s32[]{:S(2)}) async-start(), calls=%async_computation.6 | async-start | bytes 2359296 | tf_op jit(solution)/shard_map/all_gather | solution.py:57
  308.3 165.0 %all-reduce.6.cloned.1.call-start = ((), (), s32[]{:S(2)}) async-start(), calls=%async_computation.7 | async-start | bytes 4194304 | tf_op jit(solution)/shard_map/psum | solution.py:11
  358.5 33.4 %copy-start.1 = (f32[2,2048,128]{2,1,0:T(8,128)S(1)}, f32[2,2048,128]{2,1,0:T(8,128)}, u32[]{:S(2)}) copy-start(f32[2,2048,128]{2,1,0:T(8,128)} %all-gather.5.cloned.1.call-done) | copy-start | bytes 6291460
  358.5 49.7 %slice-start = ((s8[16777216]{0:T(1024)(128)(4,1)}), s8[4194304]{0:T(1024)(128)(4,1)S(1)}, s32[]{:S(2)}) async-start(s8[16777216]{0:T(1024)(128)(4,1)} %bitcast.99), calls=%async_computation.8 | async-start | bytes 8388608
  358.5 49.7 %slice-start.1 = ((s8[16777216]{0:T(1024)(128)(4,1)}), s8[4194304]{0:T(1024)(128)(4,1)S(1)}, s32[]{:S(2)}) async-start(s8[16777216]{0:T(1024)(128)(4,1)} %bitcast.99), calls=%async_computation.9 | async-start | bytes 8388608
  374.6 33.6 %slice-start.2 = ((s8[16777216]{0:T(1024)(128)(4,1)}), s8[4194304]{0:T(1024)(128)(4,1)S(1)}, s32[]{:S(2)}) async-start(s8[16777216]{0:T(1024)(128)(4,1)} %bitcast.99), calls=%async_computation.10 | async-start | bytes 8388608
  391.9 16.3 %slice-start.3 = ((s8[16777216]{0:T(1024)(128)(4,1)}), s8[4194304]{0:T(1024)(128)(4,1)S(1)}, s32[]{:S(2)}) async-start(s8[16777216]{0:T(1024)(128)(4,1)} %bitcast.99), calls=%async_computation.11 | async-start | bytes 8388608
Sparse Core Ops, SparseCore 0:
  41.3 71.0 reduce-scatter.2
  114.6 48.1 all-gather.2
  165.6 34.8 all-reduce.3
  239.5 68.7 reduce-scatter.4
  310.3 48.1 all-gather.4
  423.3 49.9 all-reduce.5
where the time goes:
time: 490 us; the launch traced here: 484 us
  waiting for transfers between devices  326 us (67%)
  matrix products  132 us (27%)
  between operations  14 us (3%)
  other arithmetic  12.1 us (2%)
    reduce_scatter x2, waiting for transfers between devices, reduce_cols(): lax.psum_scatter(partial_value, 'col', scatter_dimension=1, tiled=True)  140 us
    all_gather x2, waiting for transfers between devices, reduce_cols(): return lax.all_gather(share, 'col', axis=1, tiled=True)  100 us
    psum x2, waiting for transfers between devices, broadcast(): return lax.psum(block, axis)  85.1 us
    dot_general x8, matrix products, plain_dot(): jnp.dot(left, right, precision=lax.Precision.HIGHEST, preferred_element_t...  69 us
    dot_general x4, matrix products, adjoint_dot(): lax.dot_general(left, right, (((0,), (0,)), ((), ())), precision=lax.Prec...  63.1 us
  transfers between devices with their start and end apart: 6, of which 6 were waited for; matrix products, arithmetic and copies ran while one was open for 0% of the time, Pallas kernels for 0%

commit v1 on v0

--- a/solution.py
+++ b/solution.py
@@ -8,7 +8,7 @@
 
 def broadcast(block, axis, owner):
     block = jnp.where(lax.axis_index(axis) == owner, block, jnp.zeros_like(block))
-    return lax.psum(block, axis)
+    return jnp.sum(lax.all_gather(block, axis), axis=0)
 
 
 def plain_dot(left, right):

time: 490 us -> 477 us (0.973)
  matrix products: 132 us -> 98.7 us
  waiting for transfers between devices: 326 us -> 342 us
    all_gather x0 -> x2, waiting for transfers between devices: none -> 68.3 us  [broadcast(): return jnp.sum(lax.all_gather(block, axis), axis=0)]
    psum x2 -> x1, waiting for transfers between devices: 85.1 us -> 33.8 us  [backward(): return lax.psum(complex_product(pieces, vector, True), 'row')]
    dot_general x4, matrix products: 63.1 us -> 29.8 us  [adjoint_dot(): lax.dot_general(left, right, (((0,), (0,)), ((), ())), precision=lax.Prec...]
    reduce_sum x0 -> x2, other arithmetic: none -> 5.05 us  [broadcast(): return jnp.sum(lax.all_gather(block, axis), axis=0)]
  transfers between devices with their start and end apart: 6 -> 7, of which waited for: 6 -> 7; matrix products, arithmetic and copies ran while one was open for 0% -> 0% of each run, Pallas kernels for 0% -> 0%
where the time goes in v1:
time: 477 us; the launch traced here: 471 us
  waiting for transfers between devices  342 us (72%)
  matrix products  98.7 us (21%)
  other arithmetic  14.4 us (3%)
  between operations  14 us (3%)
    reduce_scatter x2, waiting for transfers between devices, reduce_cols(): lax.psum_scatter(partial_value, 'col', scatter_dimension=1, tiled=True)  140 us
    all_gather x2, waiting for transfers between devices, reduce_cols(): return lax.all_gather(share, 'col', axis=1, tiled=True)  100 us
    dot_general x8, matrix products, plain_dot(): jnp.dot(left, right, precision=lax.Precision.HIGHEST, preferred_element_t...  68.9 us
    all_gather x2, waiting for transfers between devices, broadcast(): return jnp.sum(lax.all_gather(block, axis), axis=0)  68.3 us
    psum x1, waiting for transfers between devices, backward(): return lax.psum(complex_product(pieces, vector, True), 'row')  33.8 us
    dot_general x4, matrix products, adjoint_dot(): lax.dot_general(left, right, (((0,), (0,)), ((), ())), precision=lax.Prec...  29.8 us
  transfers between devices with their start and end apart: 7, of which 7 were waited for; matrix products, arithmetic and copies ran while one was open for 0% of the time, Pallas kernels for 0%

profile of v1, /device:TPU:0, one launch (start us, length us, event | category | flops | bytes accessed | tf_op | source)
XLA Modules:
  0.0 471.3 jit_solution(6013228064036351587)
XLA Ops:
  6.5 9.3 %fusion.12 = f32[2048,128]{1,0:T(8,128)S(1)} fusion(f32[2,2048,1024]{2,1,0:T(8,128)} %param.3, f32[2,1024,128]{2,1,0:T(8,128)} %param.5), kind=kOutput, calls=%fused_computation.12 | convolution fusion | flops 3221225472 | bytes 9961472 | tf_op jit(solution)/shard_map/dot_general | solution.py:15
  15.9 9.2 %fusion.14 = f32[2048,128]{1,0:T(8,128)S(1)} fusion(f32[2,2048,1024]{2,1,0:T(8,128)} %param.3, f32[2,1024,128]{2,1,0:T(8,128)S(1)} %copy-done.2), kind=kOutput, calls=%fused_computation.14 | convolution fusion | flops 3221225472 | bytes 9961472 | tf_op jit(solution)/shard_map/dot_general | solution.py:15
  25.1 7.0 %fusion.47 = f32[1,2048,128]{2,1,0:T(8,128)S(1)} fusion(f32[2048,128]{1,0:T(8,128)S(1)} %fusion.12, f32[2,2048,1024]{2,1,0:T(8,128)S(1)} %copy-done, f32[2,1024,128]{2,1,0:T(8,128)S(1)} %copy-done.2), kind=kOutput, calls=%fused_computation.41 | convolution fusion | flops 3221487616 | bytes 11010048 | tf_op jit(solution)/shard_map/dot_general | solution.py:15
  32.1 7.3 %fusion.41 = f32[1,2048,128]{2,1,0:T(8,128)S(1)} fusion(f32[2048,128]{1,0:T(8,128)S(1)} %fusion.14, f32[2,2048,1024]{2,1,0:T(8,128)S(1)} %copy-done, f32[2,1024,128]{2,1,0:T(8,128)S(1)} %copy-done.2), kind=kOutput, calls=%fused_computation.39 | convolution fusion | flops 3221487616 | bytes 11010048 | tf_op jit(solution)/shard_map/dot_general | solution.py:15
  39.4 1.5 pad_maximum_fusion
  40.9 0.0 reduce-scatter.3.cloned.1.call-update
  40.9 0.0 all-gather.7.cloned.1.call-start
  40.9 71.1 %reduce-scatter.3.cloned.1.call-done = f32[2,256,128]{2,1,0:T(8,128)} async-done(((f32[2,2048,128]{2,1,0:T(8,128)}), f32[2,256,128]{2,1,0:T(8,128)}) %reduce-scatter.3.cloned.1.call-update) | async-done | bytes 262160 | tf_op jit(solution)/shard_map/reduce_scatter | solution.py:56
  112.1 0.0 all-gather.7.cloned.1.call-update
  112.1 0.0 all-gather.11.cloned.1.call-start
  112.2 50.2 %all-gather.7.cloned.1.call-done = f32[2,2048,128]{2,1,0:T(8,128)} async-done(((f32[2,256,128]{2,1,0:T(8,128)}), f32[2,2048,128]{2,1,0:T(8,128)}) %all-gather.7.cloned.1.call-update) | async-done | bytes 2097168 | tf_op jit(solution)/shard_map/all_gather | solution.py:57
  162.4 1.7 slice_multiply_fusion
  164.1 1.0 fusion.75
  165.1 0.0 all-gather.11.cloned.1.call-update
  165.2 0.0 reduce-scatter.5.cloned.1.call-start
  165.2 33.1 %all-gather.11.cloned.1.call-done = f32[8,1024,128]{2,1,0:T(8,128)} async-done(((f32[2,1024,128]{2,1,0:T(8,128)}), f32[8,1024,128]{2,1,0:T(8,128)}) %all-gather.11.cloned.1.call-update) | async-done | bytes 4194320 | tf_op jit(solution)/shard_map/all_gather | solution.py:11
  198.3 2.5 reduce_sum.18
  200.8 0.1 add.34
  201.0 9.2 %fusion.4 = f32[128,2048]{0,1:T(8,128)S(1)} fusion(f32[2,2048,1024]{2,1,0:T(8,128)} %param.4, f32[2,1024,128]{2,1,0:T(8,128)S(1)} %add.34), kind=kOutput, calls=%fused_computation.4 | convolution fusion | flops 3221225472 | bytes 9961472 | tf_op jit(solution)/shard_map/dot_general | solution.py:15
  210.2 0.0 slice-start.6
  210.2 10.0 %fusion.6 = f32[128,2048]{0,1:T(8,128)S(1)} fusion(f32[2,2048,1024]{2,1,0:T(8,128)} %param.4, f32[2,1024,128]{2,1,0:T(8,128)S(1)} %add.34), kind=kOutput, calls=%fused_computation.6 | convolution fusion | flops 3221225472 | bytes 9961472 | tf_op jit(solution)/shard_map/dot_general | solution.py:15
  220.2 0.0 slice-start.7
  220.3 9.7 %fusion.59 = f32[1,2048,128]{2,1,0:T(8,128)S(1)} fusion(f32[128,2048]{0,1:T(8,128)S(1)} %fusion.4, f32[2,2048,1024]{2,1,0:T(8,128)} %param.4, f32[2,1024,128]{2,1,0:T(8,128)S(1)} %add.34), kind=kOutput, calls=%fused_computation.45 | convolution fusion | flops 3221487616 | bytes 11010048 | tf_op jit(solution)/shard_map/dot_general | solution.py:15
  230.0 7.1 %fusion.53 = f32[1,2048,128]{2,1,0:T(8,128)S(1)} fusion(f32[128,2048]{0,1:T(8,128)S(1)} %fusion.6, f32[2,2048,1024]{2,1,0:T(8,128)S(1)} %bitcast.104, f32[2,1024,128]{2,1,0:T(8,128)S(1)} %add.34), kind=kOutput, calls=%fused_computation.43 | convolution fusion | flops 3221487616 | bytes 11010048 | tf_op jit(solution)/shard_map/dot_general | solution.py:15
  237.2 1.5 pad_maximum_fusion.1
  238.6 0.0 reduce-scatter.5.cloned.1.call-update
  238.7 0.0 all-gather.9.cloned.1.call-start
  238.7 68.5 %reduce-scatter.5.cloned.1.call-done = f32[2,256,128]{2,1,0:T(8,128)} async-done(((f32[2,2048,128]{2,1,0:T(8,128)}), f32[2,256,128]{2,1,0:T(8,128)}) %reduce-scatter.5.cloned.1.call-update) | async-done | bytes 262160 | tf_op jit(solution)/shard_map/reduce_scatter | solution.py:56
  307.2 0.0 all-gather.9.cloned.1.call-update
  307.2 0.0 all-reduce.2.cloned.1.call-start
  307.3 50.1 %all-gather.9.cloned.1.call-done = f32[2,2048,128]{2,1,0:T(8,128)} async-done(((f32[2,256,128]{2,1,0:T(8,128)}), f32[2,2048,128]{2,1,0:T(8,128)}) %all-gather.9.cloned.1.call-update) | async-done | bytes 2097168 | tf_op jit(solution)/shard_map/all_gather | solution.py:57
  357.4 9.1 %fusion = f32[128,1024]{1,0:T(8,128)S(1)} fusion(f32[2,2048,1024]{2,1,0:T(8,128)} %param.3, f32[2,2048,128]{2,1,0:T(8,128)} %all-gather.9.cloned.1.call-done), kind=kOutput, calls=%fused_computation | convolution fusion | flops 3223322624 | bytes 9961472 | tf_op jit(solution)/shard_map/dot_general | solution.py:19
  366.5 0.0 slice-start.2
  366.5 8.1 %fusion.2 = f32[128,1024]{1,0:T(8,128)S(1)} fusion(f32[2,2048,1024]{2,1,0:T(8,128)} %param.3, f32[2,2048,128]{2,1,0:T(8,128)} %all-gather.9.cloned.1.call-done), kind=kOutput, calls=%fused_computation.2 | convolution fusion | flops 3223322624 | bytes 9961472 | tf_op jit(solution)/shard_map/dot_general | solution.py:19
  374.7 7.9 %fusion.68 = f32[1,1024,128]{1,2,0:T(8,128)S(1)} fusion(f32[128,1024]{1,0:T(8,128)S(1)} %fusion, f32[2,2048,1024]{2,1,0:T(8,128)} %param.3, f32[2,2048,128]{2,1,0:T(8,128)S(1)} %copy-done.1), kind=kOutput, calls=%fused_computation.52 | convolution fusion | flops 3221356544 | bytes 10485760 | tf_op jit(solution)/shard_map/dot_general | solution.py:19
  382.6 4.7 fusion.71
  387.3 1.0 pad_maximum_fusion.2
  388.4 0.0 all-reduce.2.cloned.1.call-update
  388.4 0.0 all-gather.13.cloned.1.call-start
  388.4 1.0 dynamic-slice_select_fusion
  389.5 0.0 all-gather.13.cloned.1.call-update
  389.5 33.8 %all-reduce.2.cloned.1.call-done = f32[2,1024,128]{1,2,0:T(8,128)} async-done(((f32[2,1024,128]{1,2,0:T(8,128)}), f32[2,1024,128]{1,2,0:T(8,128)}) %all-reduce.2.cloned.1.call-update) | async-done | bytes 1048592 | tf_op jit(solution)/shard_map/psum | solution.py:70
  423.3 1.3 slice_multiply_fusion.3
  424.6 35.2 %all-gather.13.cloned.1.call-done = f32[8,1024,128]{2,1,0:T(8,128)} async-done(((f32[2,1024,128]{2,1,0:T(8,128)}), f32[8,1024,128]{2,1,0:T(8,128)}) %all-gather.13.cloned.1.call-update) | async-done | bytes 4194320 | tf_op jit(solution)/shard_map/all_gather | solution.py:11
  459.9 2.5 reduce_sum.19
  462.4 0.3 copy.13
  462.7 0.2 maximum_add_fusion
  462.9 1.3 copy.14
  (22 shorter events, 0.0 us)
Async XLA Ops:
  6.5 9.3 %copy-start.2 = (f32[2,1024,128]{2,1,0:T(8,128)S(1)}, f32[2,1024,128]{2,1,0:T(8,128)}, u32[]{:S(2)}) copy-start(f32[2,1024,128]{2,1,0:T(8,128)} %param.5) | copy-start | bytes 3145732
  6.5 105.5 %reduce-scatter.3.cloned.1.call-start = ((), (), s32[]{:S(2)}) async-start(), calls=%async_computation.2 | async-start | bytes 2359296 | tf_op jit(solution)/shard_map/reduce_scatter | solution.py:56
  6.5 18.6 %copy-start = (f32[2,2048,1024]{2,1,0:T(8,128)S(1)}, f32[2,2048,1024]{2,1,0:T(8,128)}, u32[]{:S(2)}) copy-start(f32[2,2048,1024]{2,1,0:T(8,128)} %param.3) | copy-start | bytes 50331652
  40.9 121.5 %all-gather.7.cloned.1.call-start = ((), (), s32[]{:S(2)}) async-start(), calls=%async_computation.3 | async-start | bytes 2359296 | tf_op jit(solution)/shard_map/all_gather | solution.py:57
  112.1 86.2 %all-gather.11.cloned.1.call-start = ((), (), s32[]{:S(2)}) async-start(), calls=%async_computation.7 | async-start | bytes 5242880 | tf_op jit(solution)/shard_map/all_gather | solution.py:11
  165.2 142.0 %reduce-scatter.5.cloned.1.call-start = ((), (), s32[]{:S(2)}) async-start(), calls=%async_computation.4 | async-start | bytes 2359296 | tf_op jit(solution)/shard_map/reduce_scatter | solution.py:56
  201.0 29.0 %slice-start.4 = ((s8[16777216]{0:T(1024)(128)(4,1)}), s8[4194304]{0:T(1024)(128)(4,1)S(1)}, s32[]{:S(2)}) async-start(s8[16777216]{0:T(1024)(128)(4,1)} %bitcast.103), calls=%async_computation.13 | async-start | bytes 8388608
  201.0 29.0 %slice-start.5 = ((s8[16777216]{0:T(1024)(128)(4,1)}), s8[4194304]{0:T(1024)(128)(4,1)S(1)}, s32[]{:S(2)}) async-start(s8[16777216]{0:T(1024)(128)(4,1)} %bitcast.103), calls=%async_computation.14 | async-start | bytes 8388608
  210.2 19.8 %slice-start.6 = ((s8[16777216]{0:T(1024)(128)(4,1)}), s8[4194304]{0:T(1024)(128)(4,1)S(1)}, s32[]{:S(2)}) async-start(s8[16777216]{0:T(1024)(128)(4,1)} %bitcast.103), calls=%async_computation.15 | async-start | bytes 8388608
  220.2 9.8 %slice-start.7 = ((s8[16777216]{0:T(1024)(128)(4,1)}), s8[4194304]{0:T(1024)(128)(4,1)S(1)}, s32[]{:S(2)}) async-start(s8[16777216]{0:T(1024)(128)(4,1)} %bitcast.103), calls=%async_computation.16 | async-start | bytes 8388608
  238.7 118.7 %all-gather.9.cloned.1.call-start = ((), (), s32[]{:S(2)}) async-start(), calls=%async_computation.5 | async-start | bytes 2359296 | tf_op jit(solution)/shard_map/all_gather | solution.py:57
  307.2 116.1 %all-reduce.2.cloned.1.call-start = ((), (), s32[]{:S(2)}) async-start(), calls=%async_computation.6 | async-start | bytes 2097152 | tf_op jit(solution)/shard_map/psum | solution.py:70
  357.4 17.3 %copy-start.1 = (f32[2,2048,128]{2,1,0:T(8,128)S(1)}, f32[2,2048,128]{2,1,0:T(8,128)}, u32[]{:S(2)}) copy-start(f32[2,2048,128]{2,1,0:T(8,128)} %all-gather.9.cloned.1.call-done) | copy-start | bytes 6291460
  357.4 25.2 %slice-start = ((s8[16777216]{0:T(1024)(128)(4,1)}), s8[4194304]{0:T(1024)(128)(4,1)S(1)}, s32[]{:S(2)}) async-start(s8[16777216]{0:T(1024)(128)(4,1)} %bitcast.101), calls=%async_computation.9 | async-start | bytes 8388608
  357.4 25.2 %slice-start.1 = ((s8[16777216]{0:T(1024)(128)(4,1)}), s8[4194304]{0:T(1024)(128)(4,1)S(1)}, s32[]{:S(2)}) async-start(s8[16777216]{0:T(1024)(128)(4,1)} %bitcast.101), calls=%async_computation.10 | async-start | bytes 8388608
  366.5 16.1 %slice-start.2 = ((s8[16777216]{0:T(1024)(128)(4,1)}), s8[4194304]{0:T(1024)(128)(4,1)S(1)}, s32[]{:S(2)}) async-start(s8[16777216]{0:T(1024)(128)(4,1)} %bitcast.101), calls=%async_computation.11 | async-start | bytes 8388608
  374.7 7.9 %slice-start.3 = ((s8[16777216]{0:T(1024)(128)(4,1)}), s8[4194304]{0:T(1024)(128)(4,1)S(1)}, s32[]{:S(2)}) async-start(s8[16777216]{0:T(1024)(128)(4,1)} %bitcast.101), calls=%async_computation.12 | async-start | bytes 8388608
  388.4 71.5 %all-gather.13.cloned.1.call-start = ((), (), s32[]{:S(2)}) async-start(), calls=%async_computation.8 | async-start | bytes 5242880 | tf_op jit(solution)/shard_map/all_gather | solution.py:11
Sparse Core Ops, SparseCore 0:
  41.0 71.0 reduce-scatter.2
  114.3 48.0 all-gather.6
  165.3 32.9 all-gather.10
  238.8 68.3 reduce-scatter.4
  309.2 48.0 all-gather.8
  388.5 34.7 all-reduce.1
  424.9 34.9 all-gather.12
